TPU v7x, 32 devices: a whole 2x2x4 slice. The times are simulated.
32 devices in a mesh: stn: 8 (over z, x), chan: 4 (over y, core).
Axes of the slice: x: 2, y: 2, z: 4, core: 2. Of those that a mesh axis runs over, the one named last changes fastest.
Arguments:
- samples: bfloat16 [64, 17, 2, 8192], P(('stn', 'chan')), may hold values from -6 to 6
- keeper: int32 [8, 8], replicated, may hold values from 0 to 1, as said below
Outputs:
- visibilities: bfloat16 [64, 2, 4096, 40], P('stn', None, 'chan')
Inputs may be any that keep to these rules, and one draw needn't show every extreme that they name: keeper[g, g] is 1; for g != h with d = (g - h) mod 8: keeper[g, h] is 1 where 0 < d < 4, 0 where d > 4, and at d = 4 exactly one of keeper[g, h] and keeper[h, g] is 1, which one drawn for each such pair; half of the rows hold 5 ones, the others 5 - 1.
All inputs are finite; a program needn't handle non-finite values.
Results may differ from a plain program's by a relative error of at most 0.0077.
Values may be sent and summed in bfloat16 or wider, within the bound.
A program may use at most 192 MiB of HBM per device.

v0:
```python
import math
import jax
import jax.numpy as jnp
from jax import lax
from jax.sharding import PartitionSpec as P

NFFT = 8192
TAPS = 16
CH_WIN = 1024
DFT_BLOCK = 256


def from_behind(value, axis, by):
    devices = lax.axis_size(axis)
    return lax.ppermute(value, axis, [(i, (i + by) % devices) for i in range(devices)])


def taps_table():
    pos = jnp.arange(TAPS * NFFT).astype(jnp.float32)
    shifted = (pos + 0.5) / NFFT - TAPS / 2.0
    window = 0.5 - 0.5 * jnp.cos(2.0 * math.pi * (pos + 0.5) / (TAPS * NFFT))
    return (jnp.sinc(shifted) * window).reshape(TAPS, NFFT)


def twiddles(width):
    index_n = jnp.arange(NFFT, dtype=jnp.int32)[:, None]
    index_k = jnp.arange(width, dtype=jnp.int32)[None, :]
    phase = (index_n * index_k % NFFT).astype(jnp.float32) * (2.0 * math.pi / NFFT)
    cosines = jnp.cos(phase).astype(jnp.bfloat16)
    sines = jnp.sin(phase).astype(jnp.bfloat16)
    upper = jnp.concatenate([cosines, -sines], axis=1)
    lower = jnp.concatenate([sines, cosines], axis=1)
    return jnp.concatenate([upper, lower], axis=0)


def rotations(ch_tot, width):
    blocks = ch_tot // width
    index_n = jnp.arange(NFFT, dtype=jnp.int32)[None, :]
    index_b = jnp.arange(blocks, dtype=jnp.int32)[:, None]
    phase = (index_n * index_b * width % NFFT).astype(jnp.float32) * (2.0 * math.pi / NFFT)
    return (jnp.cos(phase), jnp.sin(phase))


def channelise(block, taps, table, cos_rot, sin_rot, ch_tot):
    frames = block.shape[1] - TAPS + 1
    count = block.shape[0]
    width = table.shape[1] // 2
    blocks = ch_tot // width
    total = taps[0] * block[:, 0:frames].astype(jnp.float32)
    for tap in range(1, TAPS):
        total = total + taps[tap] * block[:, tap : tap + frames].astype(jnp.float32)
    real_part = total[:, :, 0][None]
    imag_part = total[:, :, 1][None]
    cosine = cos_rot[:, None, None, :]
    sine = sin_rot[:, None, None, :]
    rot_real = real_part * cosine + imag_part * sine
    rot_imag = imag_part * cosine - real_part * sine
    lhs = jnp.stack([rot_real, rot_imag], axis=3).astype(jnp.bfloat16)
    lhs = lhs.reshape(blocks * count * frames, 2 * NFFT)
    spectrum = jnp.dot(lhs, table, preferred_element_type=jnp.float32) * (1.0 / math.sqrt(NFFT))
    spectrum = spectrum.astype(jnp.bfloat16).reshape(blocks, count, frames, 2, width)
    spectrum = jnp.transpose(spectrum, (1, 0, 4, 3, 2))
    return spectrum.reshape(count, ch_tot, 2, frames)


def correlate(own, others, frames):
    half = others.shape[2] // 2
    turned = jnp.concatenate([-others[:, :, half:], others[:, :, :half]], axis=2)
    rhs = jnp.concatenate([others, turned], axis=0)
    product = lax.dot_general(
        own, rhs, (((2,), (2,)), ((1,), (1,))), preferred_element_type=jnp.float32
    )
    rows = others.shape[0]
    product = product.reshape(product.shape[0], product.shape[1], 2, rows)
    return jnp.transpose(product, (1, 2, 0, 3)) / frames


def slot_table(keep_rows, keep_slots):
    ranking = jnp.cumsum(keep_rows, axis=1) - 1
    slot_index = jnp.arange(keep_slots, dtype=jnp.int32)
    matched = (keep_rows[:, :, None] == 1) & (ranking[:, :, None] == slot_index[None, None, :])
    column_ids = jnp.arange(keep_rows.shape[1], dtype=jnp.int32)
    slot_column = jnp.sum(jnp.where(matched, column_ids[None, :, None], 0), axis=1)
    filled = jnp.any(matched, axis=1)
    return (slot_column, filled)


def per_device(samples, keeper):
    n_chan = lax.axis_size("chan")
    n_stn = lax.axis_size("stn")
    ch_tot = CH_WIN * n_chan
    frames = samples.shape[1] - TAPS + 1
    cos_rot, sin_rot = rotations(ch_tot, DFT_BLOCK)
    spectrum = channelise(samples, taps_table(), twiddles(DFT_BLOCK), cos_rot, sin_rot, ch_tot)
    local = lax.all_to_all(spectrum, "chan", split_axis=1, concat_axis=0, tiled=True)
    group_in = local.shape[0]
    own = local.reshape(group_in, CH_WIN, 2 * frames)
    keep_slots = n_stn // 2 + 1
    group_index = lax.axis_index("stn")
    row_keep = jnp.take(keeper, group_index, axis=0)
    slot_column, filled = slot_table(row_keep[None], keep_slots)
    slot_column = slot_column[0]
    filled = filled[0]
    nothing = jnp.zeros((), jnp.bfloat16)
    half = n_stn // 2
    stacked = own[None]
    stride = 1
    while stride < half:
        moved = from_behind(stacked, "stn", stride)
        stacked = jnp.concatenate([stacked, moved], axis=0)
        stride = stride * 2
    far_group = from_behind(own, "stn", half)
    partners = jnp.concatenate([stacked, far_group[None]], axis=0)
    partners = partners.reshape((half + 1) * group_in, CH_WIN, 2 * frames)
    tiles = correlate(own, partners, frames).astype(jnp.bfloat16)
    tiles = tiles.reshape(group_in, 2, CH_WIN, half + 1, group_in)
    slot_distance = jnp.minimum((group_index - slot_column) % n_stn, half)
    picked = jnp.take(tiles, slot_distance, axis=3)
    picked = jnp.where(filled[None, None, None, :, None], picked, nothing)
    return picked.reshape(group_in, 2, CH_WIN, keep_slots * group_in)


def solution(mesh):
    placed = (P(("stn", "chan"), None, None, None), P())
    return jax.shard_map(
        per_device,
        mesh=mesh,
        in_specs=placed,
        out_specs=P("stn", None, "chan", None),
        check_vma=False,
    )
```

profile of v0, /device:TPU:0, one launch (start us, length us, event | category | flops | bytes accessed | tf_op | source)
XLA Modules:
  0.0 166.4 jit_solution(14174221383164325046)
XLA Ops:
  0.0 2.4 %fusion.29 = f32[131072]{0:T(1024)S(1)} fusion(), kind=kLoop, calls=%fused_computation.45 | loop fusion | flops 5373952 | bytes 524288 | tf_op jit(solution)/shard_map/mul | solution.py:22
  2.4 2.1 %fusion.41 = (f32[16,8192]{1,0:T(8,128)S(1)}, f32[16,8192]{1,0:T(8,128)S(1)}) fusion(), kind=kLoop, calls=%fused_computation.65 | loop fusion | flops 1966080 | bytes 1048576 | tf_op jit(solution)/shard_map/sin | solution.py:41
  4.5 35.0 %sine_convert_fusion = (bf16[8192,256]{1,0:T(8,128)(2,1)}, bf16[8192,256]{1,0:T(8,128)(2,1)}) fusion(), kind=kLoop, calls=%fused_computation.15 | loop fusion | flops 33554432 | bytes 8388608 | tf_op jit(solution)/shard_map/convert_element_type | solution.py:30
  39.5 0.0 copy-start
  39.5 32.3 %fusion.14 = bf16[8192,256]{1,0:T(8,128)(2,1)} fusion(), kind=kLoop, calls=%fused_computation.24 | loop fusion | flops 37748736 | bytes 4194304 | tf_op jit(solution)/shard_map/neg | solution.py:31
  71.9 0.0 copy-done
  71.9 2.1 %multiply_add_fusion.1 = f32[2,2,2,8192]{3,2,1,0:T(2,128)S(1)} fusion(bf16[2,17,2,8192]{3,2,1,0:T(2,128)(2,1)S(1)} %copy-done, f32[8192]{0:T(1024)S(1)} %get-tuple-element.19, f32[8192]{0:T(1024)S(1)} %get-tuple-element.20, f32[8192]{0:T(1024)S(1)} %get-tuple-element.21, f32[8192]{0:T(1024)S(1)} %get-tuple-element.22, f32[8192]{0:T(1024)S(1)} %get-tuple-element.23, ...), kind=kLoop, calls=%fused_computation.67 | loop fusion | flops 3080192 | bytes 2883584 | tf_op jit(solution)/shard_map/add | solution.py:51
  74.0 0.2 fusion.53
  74.2 0.2 copy_bitcast_fusion.1
  74.4 4.4 %add_convert_fusion = (bf16[16,2,2,1,8192]{4,3,2,1,0:T(2,128)(2,1)S(1)}, bf16[16,2,2,1,8192]{4,3,2,1,0:T(2,128)(2,1)S(1)}) fusion(f32[16,8192]{1,0:T(8,128)S(1)} %get-tuple-element.40, f32[2,2,8192]{2,1,0:T(2,128)S(1)} %get-tuple-element.38, f32[16,8192]{1,0:T(8,128)S(1)} %get-tuple-element.41, f32[2,2,8192]{2,1,0:T(2,128)S(1)} %get-tuple-element.39), kind=kLoop, calls=%fused_computation.23 | loop fusion | flops 4194304 | bytes 3407872 | tf_op jit(solution)/shard_map/convert
  78.8 4.8 %pad_maximum_fusion = bf16[16,2,2,2,8192]{4,3,2,1,0:T(2,128)(2,1)S(1)} fusion(bf16[16,2,2,1,8192]{4,3,2,1,0:T(2,128)(2,1)S(1)} %get-tuple-element.17, bf16[16,2,2,1,8192]{4,3,2,1,0:T(2,128)(2,1)S(1)} %get-tuple-element.16), kind=kLoop, calls=%fused_computation.21 | loop fusion | flops 4194304 | bytes 4194304 | tf_op jit(solution)/shard_map/stack | solution.py:58
  83.7 1.2 copy.55
  84.8 13.7 %fusion.19 = bf16[64,512]{1,0:T(8,128)(2,1)S(1)} fusion(bf16[64,16384]{1,0:T(8,128)(2,1)S(1)} %bitcast.50, bf16[8192,256]{1,0:T(8,128)(2,1)} %get-tuple-element.43, bf16[8192,256]{1,0:T(8,128)(2,1)} %get-tuple-element.42, bf16[8192,256]{1,0:T(8,128)(2,1)} %fusion.14), kind=kOutput, calls=%fused_computation.28 | convolution fusion | flops 1140916224 | bytes 14745600 | tf_op jit(solution)/shard_map/dot_general | solution.py:60
  98.6 4.9 %copy.50 = bf16[2,16,256,2,2]{4,3,0,2,1:T(2,128)(2,1)} copy(bf16[2,16,256,2,2]{2,1,4,3,0:T(8,128)(2,1)S(1)} %bitcast.51) | data formatting | bytes 131072 | tf_op jit(solution)/shard_map/reshape | solution.py:63
  103.6 7.8 %reshape.394 = bf16[4,2,4096]{2,1,0:T(2,128)(2,1)} reshape(bf16[4096,2,2,2]{3,2,1,0:T(2,128)(2,1)} %bitcast.46) | data formatting | bytes 131072
  111.3 4.3 %all-to-all-start = ((bf16[4,2,4096]{2,1,0:T(2,128)(2,1)}), bf16[4,2,4096]{2,1,0:T(2,128)(2,1)S(1)}, u32[]{:S(2)}, u32[]{:S(2)}) async-start(bf16[4,2,4096]{2,1,0:T(2,128)(2,1)} %reshape.394), calls=%async_computation | async-start | bytes 131072 | tf_op jit(solution)/shard_map/all_to_all | solution.py:95
  115.6 0.7 fusion.51
  116.3 0.7 compare_bitcast_fusion
  117.0 0.2 reduce-window.7
  117.2 0.2 select_reduce_fusion
  117.4 2.3 %all-to-all-done = bf16[4,2,4096]{2,1,0:T(2,128)(2,1)S(1)} async-done(((bf16[4,2,4096]{2,1,0:T(2,128)(2,1)}), bf16[4,2,4096]{2,1,0:T(2,128)(2,1)S(1)}, u32[]{:S(2)}, u32[]{:S(2)}) %all-to-all-start) | async-done | bytes 65568 | tf_op jit(solution)/shard_map/all_to_all | solution.py:95
  119.7 10.0 %reshape.395 = bf16[4096,2,2,2]{3,2,1,0:T(2,128)(2,1)} reshape(bf16[4,2,4096]{2,1,0:T(2,128)(2,1)S(1)} %all-to-all-done) | data formatting | bytes 131072
  129.7 9.7 %copy.51 = bf16[2,4,1024,2,2]{2,1,4,3,0:T(4,128)(2,1)S(1)} copy(bf16[2,4,1024,2,2]{4,3,0,2,1:T(2,128)(2,1)} %bitcast.47) | data formatting | bytes 131072 | tf_op jit(solution)/shard_map/all_to_all | solution.py:95
  139.5 0.1 copy.41
  139.6 2.0 %collective-permute-start = (bf16[1,8,1024,4]{2,1,3,0:T(8,128)(2,1)S(1)}, bf16[1,8,1024,4]{2,1,3,0:T(8,128)(2,1)S(1)}, u32[]{:S(2)}, u32[]{:S(2)}) collective-permute-start(bf16[1,8,1024,4]{2,1,3,0:T(8,128)(2,1)S(1)} %broadcast_in_dim_reshape.3), channel_id=1, source_target_pairs={{0,4},{4,8},{8,12},{12,16},{16,20},{20,24},{24,28},{28,0},{1,5},{5... | collective-permute-start | bytes 196616 | tf_op jit(solution)/shard_map/ppermute | solution.py:15
  141.6 5.3 %collective-permute-done = bf16[1,8,1024,4]{2,1,3,0:T(8,128)(2,1)S(1)} collective-permute-done((bf16[1,8,1024,4]{2,1,3,0:T(8,128)(2,1)S(1)}, bf16[1,8,1024,4]{2,1,3,0:T(8,128)(2,1)S(1)}, u32[]{:S(2)}, u32[]{:S(2)}) %collective-permute-start) | collective-permute-done | bytes 65568 | tf_op jit(solution)/shard_map/ppermute | solution.py:15
  146.9 0.1 collective-permute-start.1
  147.0 0.2 fusion.43
  147.2 0.1 broadcast_in_dim.75
  147.2 0.1 broadcast_in_dim.76
  147.3 0.1 broadcast_in_dim.70
  147.4 0.1 broadcast_in_dim.71
  147.5 2.6 %collective-permute-start.2 = (bf16[8,1024,4]{1,0,2:T(8,128)(2,1)S(1)}, bf16[8,1024,4]{1,0,2:T(8,128)(2,1)S(1)}, u32[]{:S(2)}, u32[]{:S(2)}) collective-permute-start(bf16[8,1024,4]{1,0,2:T(8,128)(2,1)S(1)} %reshape.350), channel_id=1, source_target_pairs={{0,16},{4,20},{8,24},{12,28},{16,0},{20,4},{24,8},{28,12},{1,17},{... | collective-permute-start | bytes 196616 | tf_op jit(solution)/shard_map/ppermute | solution.py:15
  150.1 1.4 copy.46
  151.5 4.0 %collective-permute-done.2 = bf16[8,1024,4]{1,0,2:T(8,128)(2,1)S(1)} collective-permute-done((bf16[8,1024,4]{1,0,2:T(8,128)(2,1)S(1)}, bf16[8,1024,4]{1,0,2:T(8,128)(2,1)S(1)}, u32[]{:S(2)}, u32[]{:S(2)}) %collective-permute-start.2) | collective-permute-done | bytes 65568 | tf_op jit(solution)/shard_map/ppermute | solution.py:15
  155.5 0.0 collective-permute-done.1
  155.5 1.4 copy.44
  157.0 1.4 copy.45
  158.4 3.8 %multiply_convert_fusion = bf16[1024,8,80]{2,1,0:T(8,128)(2,1)S(1)} fusion(bf16[8,1024,4]{0,2,1:T(4,128)(2,1)} %copy.46, bf16[40,1024,4]{0,2,1:T(4,128)(2,1)} %copy.45, bf16[40,1024,4]{0,2,1:T(4,128)(2,1)} %copy.44), kind=kOutput, calls=%fused_computation.20 | convolution fusion | flops 7864320 | bytes 2031616 | tf_op jit(solution)/shard_map/dot_general | solution.py:70
  162.2 2.0 %copy.47 = bf16[1024,8,80]{0,2,1:T(8,128)(2,1)S(1)} copy(bf16[1024,8,80]{2,1,0:T(8,128)(2,1)S(1)} %multiply_convert_fusion) | data formatting | bytes 2621440 | tf_op jit(solution)/shard_map/convert_element_type | solution.py:115
  164.2 0.1 copy.48
  164.3 0.6 gather_fusion
  165.0 1.5 fusion.15
  (13 shorter events, 0.3 us)
Async XLA Ops:
  39.5 32.4 %copy-start = (bf16[2,17,2,8192]{3,2,1,0:T(2,128)(2,1)S(1)}, bf16[2,17,2,8192]{3,2,1,0:T(2,128)(2,1)}, u32[]{:S(2)}) copy-start(bf16[2,17,2,8192]{3,2,1,0:T(2,128)(2,1)} %param.2) | copy-start | bytes 3342340
  111.3 8.4 %all-to-all-start = ((bf16[4,2,4096]{2,1,0:T(2,128)(2,1)}), bf16[4,2,4096]{2,1,0:T(2,128)(2,1)S(1)}, u32[]{:S(2)}, u32[]{:S(2)}) async-start(bf16[4,2,4096]{2,1,0:T(2,128)(2,1)} %reshape.394), calls=%async_computation | async-start | bytes 131072 | tf_op jit(solution)/shard_map/all_to_all | solution.py:95
  139.6 7.3 %collective-permute-start = (bf16[1,8,1024,4]{2,1,3,0:T(8,128)(2,1)S(1)}, bf16[1,8,1024,4]{2,1,3,0:T(8,128)(2,1)S(1)}, u32[]{:S(2)}, u32[]{:S(2)}) collective-permute-start(bf16[1,8,1024,4]{2,1,3,0:T(8,128)(2,1)S(1)} %broadcast_in_dim_reshape.3), channel_id=1, source_target_pairs={{0,4},{4,8},{8,12},{12,16},{16,20},{20,24},{24,28},{28,0},{1,5},{5... | collective-permute-start | bytes 196616 | tf_op jit(solution)/shard_map/ppermute | solution.py:15
  146.9 8.6 %collective-permute-start.1 = (bf16[2,8,1024,4]{2,1,3,0:T(8,128)(2,1)S(1)}, bf16[2,8,1024,4]{2,1,3,0:T(8,128)(2,1)S(1)}, u32[]{:S(2)}, u32[]{:S(2)}) collective-permute-start(bf16[2,8,1024,4]{2,1,3,0:T(8,128)(2,1)S(1)} %pad_maximum_fusion.3), channel_id=1, source_target_pairs={{0,8},{4,12},{8,16},{12,20},{16,24},{20,28},{24,0},{28,4},{1,9},{5... | collective-permute-start | bytes 393224 | tf_op jit(solution)/shard_map/ppermute | solution.py:15
  147.5 8.0 %collective-permute-start.2 = (bf16[8,1024,4]{1,0,2:T(8,128)(2,1)S(1)}, bf16[8,1024,4]{1,0,2:T(8,128)(2,1)S(1)}, u32[]{:S(2)}, u32[]{:S(2)}) collective-permute-start(bf16[8,1024,4]{1,0,2:T(8,128)(2,1)S(1)} %reshape.350), channel_id=1, source_target_pairs={{0,16},{4,20},{8,24},{12,28},{16,0},{20,4},{24,8},{28,12},{1,17},{... | collective-permute-start | bytes 196616 | tf_op jit(solution)/shard_map/ppermute | solution.py:15
where the time goes:
time: 167 us; the launch traced here: 166 us
  other arithmetic  86.7 us (52%)
  local copies, waits for them, and re-layouts  41.5 us (25%)
  matrix products  17.5 us (10%)
  waiting for transfers between devices  11.6 us (7%)
  starting transfers between devices  8.94 us (5%)
    convert_element_type x1, other arithmetic, twiddles(): sines = jnp.sin(phase).astype(jnp.bfloat16)  35 us
    neg x1, other arithmetic, twiddles(): upper = jnp.concatenate([cosines, -sines], axis=1)  32.3 us
    unnamed x6, local copies, waits for them, and re-layouts  19.2 us
    dot_general x1, matrix products, channelise(): jnp.dot(lhs, table, preferred_element_type=jnp.float32)  13.7 us
    all_to_all x2, local copies, waits for them, and re-layouts, per_device(): lax.all_to_all(spectrum, 'chan', split_axis=1, concat_axis=0, tiled=True)  9.8 us
    ppermute x3, waiting for transfers between devices, from_behind(): lax.ppermute(value, axis, [(i, (i + by) % devices) for i in range(devices)])  9.25 us
    reshape x1, local copies, waits for them, and re-layouts, channelise(): return spectrum.reshape(count, ch_tot, 2, frames)  4.94 us
    another operation x1, other arithmetic, channelise(): lhs = jnp.stack([rot_real, rot_imag], axis=3).astype(jnp.bfloat16)  4.84 us
  transfers between devices with their start and end apart: 4, of which 3 were waited for; matrix products, arithmetic and copies ran while one was open for 2% of the time, Pallas kernels for 0%

commit v1 on v0

--- a/solution.py
+++ b/solution.py
@@ -8,6 +8,29 @@
 TAPS = 16
 CH_WIN = 1024
 DFT_BLOCK = 256
+
+
+def cut_along(value, dim, size):
+    before, after = (value.shape[:dim], value.shape[dim + 1 :])
+    return jnp.moveaxis(value.reshape(*before, size, -1, *after), dim, 0)
+
+
+def in_order(pieces, dim):
+    pieces = jnp.moveaxis(pieces, 0, dim)
+    shape = pieces.shape
+    return pieces.reshape(*shape[:dim], shape[dim] * shape[dim + 1], *shape[dim + 2 :])
+
+
+def exchange_directly(array, axis, split_dim, concat_dim):
+    size, index = (lax.axis_size(axis), lax.axis_index(axis))
+    parts = cut_along(array, split_dim, size)
+    result = parts
+    for step in range(1, size):
+        target, source = ((index + step) % size, (index - step) % size)
+        sent = lax.dynamic_index_in_dim(parts, target, 0)
+        other = lax.ppermute(sent, axis, [(i, (i + step) % size) for i in range(size)])
+        result = lax.dynamic_update_slice_in_dim(result, other, source, axis=0)
+    return in_order(result, concat_dim)
 
 
 def from_behind(value, axis, by):
@@ -92,7 +115,7 @@
     frames = samples.shape[1] - TAPS + 1
     cos_rot, sin_rot = rotations(ch_tot, DFT_BLOCK)
     spectrum = channelise(samples, taps_table(), twiddles(DFT_BLOCK), cos_rot, sin_rot, ch_tot)
-    local = lax.all_to_all(spectrum, "chan", split_axis=1, concat_axis=0, tiled=True)
+    local = exchange_directly(spectrum, "chan", 1, 0)
     group_in = local.shape[0]
     own = local.reshape(group_in, CH_WIN, 2 * frames)
     keep_slots = n_stn // 2 + 1

time: 167 us -> 133 us (0.80)
  local copies, waits for them, and re-layouts: 41.5 us -> 9.68 us
  waiting for transfers between devices: 11.6 us -> 9.77 us
    unnamed x6 -> x4, local copies, waits for them, and re-layouts: 19.2 us -> 1.37 us
    all_to_all x2 -> x0, local copies, waits for them, and re-layouts: 9.8 us -> none  [per_device(): lax.all_to_all(spectrum, 'chan', split_axis=1, concat_axis=0, tiled=True)]
    reshape x3 -> x0, local copies, waits for them, and re-layouts: 6.33 us -> none  [the longest x1 4.94 us: channelise(): return spectrum.reshape(count, ch_tot, 2, frames)]
    ppermute x0 -> x3, starting transfers between devices: none -> 4.51 us  [exchange_directly(): lax.ppermute(sent, axis, [(i, (i + step) % size) for i in range(size)])]
    all_to_all x1 -> x0, starting transfers between devices: 4.26 us -> none  [per_device(): lax.all_to_all(spectrum, 'chan', split_axis=1, concat_axis=0, tiled=True)]
    all_to_all x1 -> x0, waiting for transfers between devices: 2.33 us -> none  [per_device(): lax.all_to_all(spectrum, 'chan', split_axis=1, concat_axis=0, tiled=True)]
  transfers between devices with their start and end apart: 4 -> 6, of which waited for: 3 -> 2; matrix products, arithmetic and copies ran while one was open for 2% -> 3% of each run, Pallas kernels for 0% -> 0%
where the time goes in v1:
time: 133 us
  other arithmetic  86.8 us (65%)
  matrix products  17.5 us (13%)
  waiting for transfers between devices  9.77 us (7%)
  local copies, waits for them, and re-layouts  9.68 us (7%)
  starting transfers between devices  8.53 us (6%)
    convert_element_type x1, other arithmetic, twiddles(): sines = jnp.sin(phase).astype(jnp.bfloat16)  35.1 us
    neg x1, other arithmetic, twiddles(): upper = jnp.concatenate([cosines, -sines], axis=1)  32.4 us
    dot_general x1, matrix products, channelise(): jnp.dot(lhs, table, preferred_element_type=jnp.float32)  13.7 us
    ppermute x3, waiting for transfers between devices, from_behind(): lax.ppermute(value, axis, [(i, (i + by) % devices) for i in range(devices)])  9.77 us
    another operation x1, other arithmetic, channelise(): lhs = jnp.stack([rot_real, rot_imag], axis=3).astype(jnp.bfloat16)  4.84 us
    another operation x2, other arithmetic  4.58 us
    ppermute x3, starting transfers between devices, exchange_directly(): lax.ppermute(sent, axis, [(i, (i + step) % size) for i in range(size)])  4.51 us
    ppermute x3, starting transfers between devices, from_behind(): lax.ppermute(value, axis, [(i, (i + by) % devices) for i in range(devices)])  4.02 us
  transfers between devices with their start and end apart: 6, of which 2 were waited for; matrix products, arithmetic and copies ran while one was open for 3% of the time, Pallas kernels for 0%

profile of v1, /device:TPU:0, one launch (start us, length us, event | category | flops | bytes accessed | tf_op | source)
XLA Modules:
  0.0 132.6 jit_solution(797827355461149321)
XLA Ops:
  0.0 2.4 %fusion.29 = f32[131072]{0:T(1024)S(1)} fusion(), kind=kLoop, calls=%fused_computation.45 | loop fusion | flops 5373952 | bytes 524288 | tf_op jit(solution)/shard_map/mul | solution.py:45
  2.4 2.1 %fusion.41 = (f32[16,8192]{1,0:T(8,128)S(1)}, f32[16,8192]{1,0:T(8,128)S(1)}) fusion(), kind=kLoop, calls=%fused_computation.65 | loop fusion | flops 1966080 | bytes 1048576 | tf_op jit(solution)/shard_map/sin | solution.py:64
  4.5 35.1 %sine_convert_fusion = (bf16[8192,256]{1,0:T(8,128)(2,1)}, bf16[8192,256]{1,0:T(8,128)(2,1)}) fusion(), kind=kLoop, calls=%fused_computation.15 | loop fusion | flops 33554432 | bytes 8388608 | tf_op jit(solution)/shard_map/convert_element_type | solution.py:53
  39.5 0.0 copy-start
  39.5 32.4 %fusion.14 = bf16[8192,256]{1,0:T(8,128)(2,1)} fusion(), kind=kLoop, calls=%fused_computation.24 | loop fusion | flops 37748736 | bytes 4194304 | tf_op jit(solution)/shard_map/neg | solution.py:54
  71.9 0.0 copy-done
  71.9 2.1 %multiply_add_fusion.1 = f32[2,2,2,8192]{3,2,1,0:T(2,128)S(1)} fusion(bf16[2,17,2,8192]{3,2,1,0:T(2,128)(2,1)S(1)} %copy-done, f32[8192]{0:T(1024)S(1)} %get-tuple-element.19, f32[8192]{0:T(1024)S(1)} %get-tuple-element.20, f32[8192]{0:T(1024)S(1)} %get-tuple-element.21, f32[8192]{0:T(1024)S(1)} %get-tuple-element.22, f32[8192]{0:T(1024)S(1)} %get-tuple-element.23, ...), kind=kLoop, calls=%fused_computation.67 | loop fusion | flops 3080192 | bytes 2883584 | tf_op jit(solution)/shard_map/add | solution.py:74
  74.0 0.2 fusion.53
  74.2 0.2 copy_bitcast_fusion.1
  74.5 4.4 %add_convert_fusion = (bf16[16,2,2,1,8192]{4,3,2,1,0:T(2,128)(2,1)S(1)}, bf16[16,2,2,1,8192]{4,3,2,1,0:T(2,128)(2,1)S(1)}) fusion(f32[16,8192]{1,0:T(8,128)S(1)} %get-tuple-element.43, f32[2,2,8192]{2,1,0:T(2,128)S(1)} %get-tuple-element.41, f32[16,8192]{1,0:T(8,128)S(1)} %get-tuple-element.44, f32[2,2,8192]{2,1,0:T(2,128)S(1)} %get-tuple-element.42), kind=kLoop, calls=%fused_computation.23 | loop fusion | flops 4194304 | bytes 3407872 | tf_op jit(solution)/shard_map/convert
  78.9 4.8 %pad_maximum_fusion = bf16[16,2,2,2,8192]{4,3,2,1,0:T(2,128)(2,1)S(1)} fusion(bf16[16,2,2,1,8192]{4,3,2,1,0:T(2,128)(2,1)S(1)} %get-tuple-element.17, bf16[16,2,2,1,8192]{4,3,2,1,0:T(2,128)(2,1)S(1)} %get-tuple-element.16), kind=kLoop, calls=%fused_computation.21 | loop fusion | flops 4194304 | bytes 4194304 | tf_op jit(solution)/shard_map/stack | solution.py:81
  83.7 1.2 copy.49
  84.9 13.7 %fusion.19 = bf16[64,512]{1,0:T(8,128)(2,1)S(1)} fusion(bf16[64,16384]{1,0:T(8,128)(2,1)S(1)} %bitcast.54, bf16[8192,256]{1,0:T(8,128)(2,1)} %get-tuple-element.46, bf16[8192,256]{1,0:T(8,128)(2,1)} %get-tuple-element.45, bf16[8192,256]{1,0:T(8,128)(2,1)} %fusion.14), kind=kOutput, calls=%fused_computation.28 | convolution fusion | flops 1140916224 | bytes 14745600 | tf_op jit(solution)/shard_map/dot_general | solution.py:83
  98.7 0.1 dynamic-slice_bitcast_fusion
  98.8 0.5 collective-permute-start
  99.4 2.6 %collective-permute-start.1 = (bf16[1,2,1024,2,2]{2,0,4,3,1:T(2,128)(2,1)S(1)}, bf16[1,2,1024,2,2]{2,0,4,3,1:T(2,128)(2,1)S(1)}, u32[]{:S(2)}, u32[]{:S(2)}) collective-permute-start(bf16[1,2,1024,2,2]{2,0,4,3,1:T(2,128)(2,1)S(1)} %get-tuple-element.39), channel_id=1, source_target_pairs={{0,2},{1,3},{2,0},{3,1},{4,6},{5,7},{6,4},{7,5},{8,10},{9,11},{10,... | collective-permute-start | bytes 49160 | tf_op jit(solution)/shard_map/ppermute | solution.py:31
  101.9 1.4 %collective-permute-start.2 = (bf16[1,2,1024,2,2]{2,0,4,3,1:T(2,128)(2,1)S(1)}, bf16[1,2,1024,2,2]{2,0,4,3,1:T(2,128)(2,1)S(1)}, u32[]{:S(2)}, u32[]{:S(2)}) collective-permute-start(bf16[1,2,1024,2,2]{2,0,4,3,1:T(2,128)(2,1)S(1)} %get-tuple-element.38), channel_id=1, source_target_pairs={{0,3},{1,0},{2,1},{3,2},{4,7},{5,4},{6,5},{7,6},{8,11},{9,8},{10,9... | collective-permute-start | bytes 49160 | tf_op jit(solution)/shard_map/ppermute | solution.py:31
  103.3 0.7 fusion.51
  104.0 0.7 compare_bitcast_fusion
  104.7 0.2 reduce-window.7
  104.9 0.2 select_reduce_fusion
  105.2 0.0 collective-permute-done
  105.2 0.2 dynamic_update_slice.9
  105.4 0.0 collective-permute-done.1
  105.4 0.2 dynamic_update_slice.10
  105.6 0.0 collective-permute-done.2
  105.6 0.2 dynamic_update_slice.11
  105.7 0.1 copy.37
  105.9 1.5 %collective-permute-start.3 = (bf16[1,8,1024,4]{2,1,3,0:T(8,128)(2,1)S(1)}, bf16[1,8,1024,4]{2,1,3,0:T(8,128)(2,1)S(1)}, u32[]{:S(2)}, u32[]{:S(2)}) collective-permute-start(bf16[1,8,1024,4]{2,1,3,0:T(8,128)(2,1)S(1)} %broadcast_in_dim_reshape_reshape.3), channel_id=1, source_target_pairs={{0,4},{4,8},{8,12},{12,16},{16,20},{20,24},{24,28},{28,0},{1,5},{5... | collective-permute-start | bytes 196616 | tf_op jit(solution)/shard_map/ppermute | solution.py:38
  107.4 5.5 %collective-permute-done.3 = bf16[1,8,1024,4]{2,1,3,0:T(8,128)(2,1)S(1)} collective-permute-done((bf16[1,8,1024,4]{2,1,3,0:T(8,128)(2,1)S(1)}, bf16[1,8,1024,4]{2,1,3,0:T(8,128)(2,1)S(1)}, u32[]{:S(2)}, u32[]{:S(2)}) %collective-permute-start.3) | collective-permute-done | bytes 65568 | tf_op jit(solution)/shard_map/ppermute | solution.py:38
  112.9 0.1 collective-permute-start.4
  113.0 0.2 fusion.43
  113.1 0.1 broadcast_in_dim.75
  113.2 0.1 broadcast_in_dim.76
  113.3 0.1 broadcast_in_dim.70
  113.4 0.1 broadcast_in_dim.71
  113.5 2.4 %collective-permute-start.5 = (bf16[8,1024,4]{1,0,2:T(8,128)(2,1)S(1)}, bf16[8,1024,4]{1,0,2:T(8,128)(2,1)S(1)}, u32[]{:S(2)}, u32[]{:S(2)}) collective-permute-start(bf16[8,1024,4]{1,0,2:T(8,128)(2,1)S(1)} %reshape_reshape.7), channel_id=1, source_target_pairs={{0,16},{4,20},{8,24},{12,28},{16,0},{20,4},{24,8},{28,12},{1,17},{... | collective-permute-start | bytes 196616 | tf_op jit(solution)/shard_map/ppermute | solution.py:38
  115.9 1.4 %copy.42 = bf16[8,1024,4]{0,2,1:T(4,128)(2,1)} copy(bf16[8,1024,4]{1,0,2:T(8,128)(2,1)S(1)} %reshape_reshape.7) | data formatting | bytes 131072 | tf_op jit(solution)/shard_map/reshape;reshape | solution.py:120
  117.3 4.3 %collective-permute-done.5 = bf16[8,1024,4]{1,0,2:T(8,128)(2,1)S(1)} collective-permute-done((bf16[8,1024,4]{1,0,2:T(8,128)(2,1)S(1)}, bf16[8,1024,4]{1,0,2:T(8,128)(2,1)S(1)}, u32[]{:S(2)}, u32[]{:S(2)}) %collective-permute-start.5) | collective-permute-done | bytes 65568 | tf_op jit(solution)/shard_map/ppermute | solution.py:38
  121.6 0.0 collective-permute-done.4
  121.7 1.4 %copy.40 = bf16[40,1024,4]{0,2,1:T(4,128)(2,1)} copy(bf16[40,1024,4]{1,0,2:T(8,128)(2,1)S(1)} %copy_bitcast_fusion) | data formatting | bytes 655360 | tf_op jit(solution)/shard_map/reshape | solution.py:137
  123.1 1.4 %copy.41 = bf16[40,1024,4]{0,2,1:T(4,128)(2,1)} copy(bf16[40,1024,4]{1,0,2:T(8,128)(2,1)S(1)} %pad_maximum_fusion.2) | data formatting | bytes 655360 | tf_op jit(solution)/shard_map/concatenate | solution.py:91
  124.5 3.8 %multiply_convert_fusion = bf16[1024,8,80]{2,1,0:T(8,128)(2,1)S(1)} fusion(bf16[8,1024,4]{0,2,1:T(4,128)(2,1)} %copy.42, bf16[40,1024,4]{0,2,1:T(4,128)(2,1)} %copy.41, bf16[40,1024,4]{0,2,1:T(4,128)(2,1)} %copy.40), kind=kOutput, calls=%fused_computation.20 | convolution fusion | flops 7864320 | bytes 2031616 | tf_op jit(solution)/shard_map/dot_general | solution.py:93
  128.3 2.0 %copy.43 = bf16[1024,8,80]{0,2,1:T(8,128)(2,1)S(1)} copy(bf16[1024,8,80]{2,1,0:T(8,128)(2,1)S(1)} %multiply_convert_fusion) | data formatting | bytes 2621440 | tf_op jit(solution)/shard_map/convert_element_type | solution.py:138
  130.3 0.1 copy.44
  130.4 0.6 gather_fusion
  131.1 1.5 %fusion.15 = bf16[8,2,1024,40]{2,3,1,0:T(8,128)(2,1)} fusion(pred[40]{0:T(512)(128)(4,1)S(1)} %broadcast_in_dim.76, pred[40]{0:T(512)(128)(4,1)S(1)} %broadcast_in_dim.71, bf16[5,8,2,1024,8]{3,4,2,1,0:T(8,128)(2,1)S(1)} %gather_fusion), kind=kLoop, calls=%fused_computation.26 | loop fusion | flops 1310720 | bytes 2621520 | tf_op jit(solution)/shard_map/jit(_where)/select_n | solution.py:142
  (14 shorter events, 0.3 us)
Async XLA Ops:
  39.5 32.4 %copy-start = (bf16[2,17,2,8192]{3,2,1,0:T(2,128)(2,1)S(1)}, bf16[2,17,2,8192]{3,2,1,0:T(2,128)(2,1)}, u32[]{:S(2)}) copy-start(bf16[2,17,2,8192]{3,2,1,0:T(2,128)(2,1)} %param.2) | copy-start | bytes 3342340
  98.8 6.4 %collective-permute-start = (bf16[1,2,1024,2,2]{2,0,4,3,1:T(2,128)(2,1)S(1)}, bf16[1,2,1024,2,2]{2,0,4,3,1:T(2,128)(2,1)S(1)}, u32[]{:S(2)}, u32[]{:S(2)}) collective-permute-start(bf16[1,2,1024,2,2]{2,0,4,3,1:T(2,128)(2,1)S(1)} %get-tuple-element.40), channel_id=1, source_target_pairs={{0,1},{1,2},{2,3},{3,0},{4,5},{5,6},{6,7},{7,4},{8,9},{9,10},{10,1... | collective-permute-start | bytes 49160 | tf_op jit(solution)/shard_map/ppermute | solution.py:31
  99.4 6.0 %collective-permute-start.1 = (bf16[1,2,1024,2,2]{2,0,4,3,1:T(2,128)(2,1)S(1)}, bf16[1,2,1024,2,2]{2,0,4,3,1:T(2,128)(2,1)S(1)}, u32[]{:S(2)}, u32[]{:S(2)}) collective-permute-start(bf16[1,2,1024,2,2]{2,0,4,3,1:T(2,128)(2,1)S(1)} %get-tuple-element.39), channel_id=1, source_target_pairs={{0,2},{1,3},{2,0},{3,1},{4,6},{5,7},{6,4},{7,5},{8,10},{9,11},{10,... | collective-permute-start | bytes 49160 | tf_op jit(solution)/shard_map/ppermute | solution.py:31
  101.9 3.6 %collective-permute-start.2 = (bf16[1,2,1024,2,2]{2,0,4,3,1:T(2,128)(2,1)S(1)}, bf16[1,2,1024,2,2]{2,0,4,3,1:T(2,128)(2,1)S(1)}, u32[]{:S(2)}, u32[]{:S(2)}) collective-permute-start(bf16[1,2,1024,2,2]{2,0,4,3,1:T(2,128)(2,1)S(1)} %get-tuple-element.38), channel_id=1, source_target_pairs={{0,3},{1,0},{2,1},{3,2},{4,7},{5,4},{6,5},{7,6},{8,11},{9,8},{10,9... | collective-permute-start | bytes 49160 | tf_op jit(solution)/shard_map/ppermute | solution.py:31
  105.9 7.0 %collective-permute-start.3 = (bf16[1,8,1024,4]{2,1,3,0:T(8,128)(2,1)S(1)}, bf16[1,8,1024,4]{2,1,3,0:T(8,128)(2,1)S(1)}, u32[]{:S(2)}, u32[]{:S(2)}) collective-permute-start(bf16[1,8,1024,4]{2,1,3,0:T(8,128)(2,1)S(1)} %broadcast_in_dim_reshape_reshape.3), channel_id=1, source_target_pairs={{0,4},{4,8},{8,12},{12,16},{16,20},{20,24},{24,28},{28,0},{1,5},{5... | collective-permute-start | bytes 196616 | tf_op jit(solution)/shard_map/ppermute | solution.py:38
  112.9 8.7 %collective-permute-start.4 = (bf16[2,8,1024,4]{2,1,3,0:T(8,128)(2,1)S(1)}, bf16[2,8,1024,4]{2,1,3,0:T(8,128)(2,1)S(1)}, u32[]{:S(2)}, u32[]{:S(2)}) collective-permute-start(bf16[2,8,1024,4]{2,1,3,0:T(8,128)(2,1)S(1)} %pad_maximum_fusion.3), channel_id=1, source_target_pairs={{0,8},{4,12},{8,16},{12,20},{16,24},{20,28},{24,0},{28,4},{1,9},{5... | collective-permute-start | bytes 393224 | tf_op jit(solution)/shard_map/ppermute | solution.py:38
  113.5 8.1 %collective-permute-start.5 = (bf16[8,1024,4]{1,0,2:T(8,128)(2,1)S(1)}, bf16[8,1024,4]{1,0,2:T(8,128)(2,1)S(1)}, u32[]{:S(2)}, u32[]{:S(2)}) collective-permute-start(bf16[8,1024,4]{1,0,2:T(8,128)(2,1)S(1)} %reshape_reshape.7), channel_id=1, source_target_pairs={{0,16},{4,20},{8,24},{12,28},{16,0},{20,4},{24,8},{28,12},{1,17},{... | collective-permute-start | bytes 196616 | tf_op jit(solution)/shard_map/ppermute | solution.py:38
